TPU v7x, 512 devices: a whole 4x8x8 slice. The times are simulated.
512 devices in a mesh: pts: 64 (over x, y, core), blk: 8 (over z).
Axes of the slice: x: 4, y: 8, z: 8, core: 2. Of those that a mesh axis runs over, the one named last changes fastest.
Arguments:
- deviations: bfloat16 [3145728, 256], P(('pts', 'blk')), may hold values from -24 to 24
- basis: bfloat16 [3145728, 64], P(('pts', 'blk')), may hold values from -0.0034179688 to 0.0034179688
- sensitivity: bfloat16 [64, 512, 512], P('pts', 'blk'), may hold values from -0.75 to 0.75
- blade_ids: int32 [24], replicated, may hold values from 0 to 255, as said below
Outputs:
- gram: float32 [256, 256], P('pts', 'blk')
- change: float32 [24, 512, 512], P(None, 'blk', 'pts')
Inputs may be any that keep to these rules, and one draw needn't show every extreme that they name: `blade_ids`: distinct blade numbers; blade 0 and blade 256 - 1 are always among them.
All inputs are finite; a program needn't handle non-finite values.
Results may differ from a plain program's by a relative error of at most 0.0003.
Values may be sent and summed in bfloat16 or wider, within the bound.
No kernel may reach another device: no remote copies, remote signals or barrier semaphores. Data moves between devices by JAX's collectives and lax.ppermute only.
A program may use at most 64 MiB of HBM per device.

v0:
```python
import jax
import jax.numpy as jnp
from jax import lax
from jax.sharding import PartitionSpec as P


def on_device(deviations, basis, sensitivity, blade_ids):
    count_pts = lax.axis_size("pts")
    count_blk = lax.axis_size("blk")
    total = deviations.shape[0] * count_pts * count_blk
    blades = deviations.shape[1]
    dims = (((0,), (0,)), ((), ()))
    term = lax.dot_general(deviations, deviations, dims, preferred_element_type=jnp.float32) / total
    row_part = lax.psum_scatter(term, "pts", scatter_dimension=0, tiled=True)
    gram = lax.psum_scatter(row_part, "blk", scatter_dimension=1, tiled=True)
    coeff_part = lax.dot_general(basis, deviations, dims, preferred_element_type=jnp.float32)
    energy_part = jnp.sum(jnp.square(deviations.astype(jnp.float32)), axis=0) / total
    selector = (jnp.arange(blades, dtype=jnp.int32)[:, None] == blade_ids[None, :]).astype(
        jnp.float32
    )
    coeffs, energy = lax.psum((coeff_part, energy_part), ("pts", "blk"))
    picked = jnp.dot(coeffs, selector, precision=lax.Precision.HIGHEST)
    picked_energy = jnp.dot(energy, selector, precision=lax.Precision.HIGHEST)
    weights = picked / jnp.sqrt(picked_energy + 1e-05)
    per_dev = sensitivity.shape[0]
    start = lax.axis_index("pts") * per_dev
    local_weights = lax.dynamic_slice_in_dim(weights, start, per_dev, 0)
    partial_value = jnp.einsum(
        "kb,kij->bij",
        local_weights,
        sensitivity.astype(jnp.float32),
        precision=lax.Precision.HIGHEST,
    )
    change = lax.psum_scatter(partial_value, "pts", scatter_dimension=2, tiled=True)
    return (gram, change)


def solution(mesh):
    in_specs = (P(("pts", "blk"), None), P(("pts", "blk"), None), P("pts", "blk", None), P())
    out_specs = (P("pts", "blk"), P(None, "blk", "pts"))
    return jax.shard_map(
        on_device, mesh=mesh, in_specs=in_specs, out_specs=out_specs, check_vma=False
    )
```

profile of v0, /device:TPU:16, one launch (start us, length us, event | category | flops | bytes accessed | tf_op | source)
XLA Modules:
  0.0 672.3 jit_solution(4870297336945372544)
XLA Ops:
  7.2 0.0 copy-start
  7.2 0.0 all-reduce.4.cloned.1.call-start
  7.2 1.1 copy-done
  8.3 3.2 fusion.6
  11.5 0.0 all-reduce.4.cloned.1.call-update
  11.5 0.0 all-reduce.6.cloned.1.call-start
  11.5 4.6 convolution_multiply_fusion
  16.1 0.0 copy-start.1
  16.1 0.0 copy-start.2
  16.1 0.0 all-reduce.6.cloned.1.call-update
  16.1 0.0 reduce-scatter.7.cloned.1.call-start
  16.2 2.7 multiply_reduce_fusion
  18.9 104.8 %psum.15 = f32[256]{0:T(256)S(1)} all-reduce(f32[256]{0:T(256)S(1)} %broadcast_multiply_fusion.1), channel_id=1, replica_groups=mesh['pts'=64,'blk'=8] {'pts','blk'}, use_global_device_ids=true, to_apply=%region_4.0 | all-reduce | flops 256 | bytes 2048 | tf_op jit(solution)/shard_map/psum | solution.py:21
  123.7 0.0 copy-done.1
  123.7 0.1 copy.7
  123.8 0.0 copy-done.2
  123.8 0.2 fusion.1
  124.0 1.3 dynamic-slice
  125.9 154.2 %all-reduce.4.cloned.1.call-done = f32[64,256]{1,0:T(8,128)} async-done(((f32[64,256]{1,0:T(8,128)}), f32[64,256]{1,0:T(8,128)}) %all-reduce.4.cloned.1.call-update) | async-done | bytes 65552 | tf_op jit(solution)/shard_map/psum | solution.py:21
  280.1 1.0 fusion.2
  281.2 181.3 %all-reduce.6.cloned.1.call-done = f32[256,256]{1,0:T(8,128)} async-done(((f32[256,256]{1,0:T(8,128)}), f32[256,256]{1,0:T(8,128)}) %all-reduce.6.cloned.1.call-update) | async-done | bytes 262160
  462.5 0.7 constant_dynamic-slice_fusion
  463.2 0.8 copy.8
  464.0 0.0 reduce-scatter.7.cloned.1.call-update
  464.0 0.0 reduce-scatter.5.cloned.1.call-start
  464.1 3.4 broadcast_multiply_fusion
  467.5 0.0 reduce-scatter.5.cloned.1.call-update
  467.5 38.9 %reduce-scatter.7.cloned.1.call-done = f32[32,4]{1,0:T(8,128)} async-done(((f32[256,4]{1,0:T(8,128)}), f32[32,4]{1,0:T(8,128)}) %reduce-scatter.7.cloned.1.call-update) | async-done | bytes 528
  506.4 1.4 copy.9
  507.8 158.0 %reduce-scatter.5.cloned.1.call-done = f32[24,64,8]{1,2,0:T(8,128)} async-done(((f32[24,64,512]{1,2,0:T(8,128)}), f32[24,64,8]{1,2,0:T(8,128)}) %reduce-scatter.5.cloned.1.call-update) | async-done | bytes 49168 | tf_op jit(solution)/shard_map/reduce_scatter | solution.py:34
  (3 shorter events, 0.0 us)
Async XLA Ops:
  7.2 1.1 copy-start
  7.2 273.0 %all-reduce.4.cloned.1.call-start = ((), (), s32[]{:S(2)}) async-start(), calls=%async_computation.2 | async-start | bytes 131072 | tf_op jit(solution)/shard_map/psum | solution.py:21
  11.5 451.0 %all-reduce.6.cloned.1.call-start = ((), (), s32[]{:S(2)}) async-start(), calls=%async_computation.5 | async-start | bytes 524288
  16.1 107.6 %copy-start.1 = (bf16[1,64,512]{2,1,0:T(8,128)(2,1)S(1)}, bf16[1,64,512]{2,1,0:T(8,128)(2,1)}, u32[]{:S(2)}) copy-start(bf16[1,64,512]{2,1,0:T(8,128)(2,1)} %param.6) | copy-start | bytes 196612
  16.1 107.7 %copy-start.2 = (s32[24]{0:T(128)S(1)}, s32[24]{0:T(128)}, u32[]{:S(2)}) copy-start(s32[24]{0:T(128)} %param.7) | copy-start | bytes 292
  16.1 490.3 %reduce-scatter.7.cloned.1.call-start = ((), (), s32[]{:S(2)}) async-start(), calls=%async_computation.4 | async-start | bytes 147456
  464.0 201.7 %reduce-scatter.5.cloned.1.call-start = ((), (), s32[]{:S(2)}) async-start(), calls=%async_computation.3 | async-start | bytes 6389760 | tf_op jit(solution)/shard_map/reduce_scatter | solution.py:34
Sparse Core Ops, SparseCore 0:
  13.5 266.5 all-reduce.3
  283.6 178.8 all-reduce.5
  465.3 41.0 reduce-scatter.6
  511.6 154.1 reduce-scatter.4
where the time goes:
time: 673 us; the launch traced here: 672 us
  waiting for transfers between devices  532 us (79%)
  blocking collectives  105 us (16%)
  between operations  14.5 us (2%)
  matrix products  8.89 us (1%)
    unnamed x6, waiting for transfers between devices  220 us
    reduce_scatter x1, waiting for transfers between devices, on_device(): lax.psum_scatter(partial_value, 'pts', scatter_dimension=2, tiled=True)  158 us
    psum x1, waiting for transfers between devices, on_device(): coeffs, energy = lax.psum((coeff_part, energy_part), ('pts', 'blk'))  154 us
    psum x1, blocking collectives, on_device(): coeffs, energy = lax.psum((coeff_part, energy_part), ('pts', 'blk'))  105 us
  transfers between devices with their start and end apart: 4, of which 4 were waited for; matrix products, arithmetic and copies ran while one was open for 2% of the time, Pallas kernels for 0%

commit v1 on v0

v1 whole, which is shorter than its diff:
```python
import functools

import jax
import jax.numpy as jnp
from jax import lax
from jax.experimental import pallas as pl
from jax.experimental.pallas import tpu as pltpu
from jax.sharding import Mesh, PartitionSpec as P

F32 = jnp.float32
HIGHEST = lax.Precision.HIGHEST
VMEM = pl.BlockSpec(memory_space=pltpu.VMEM)
SMEM = pl.BlockSpec(memory_space=pltpu.SMEM)

NX, NY, NC, NZ = 4, 8, 2, 8
BLADES, SHAPES, ORDER, REAL = 256, 64, 512, 24
CHUNKS = 4


def params(mib):
    return pltpu.CompilerParams(vmem_limit_bytes=mib * 1024 * 1024)


def halves(first, second):
    axis = first.ndim - 2
    row = lax.broadcasted_iota(jnp.int32, first.shape, axis)
    upper = jnp.where(row < 4, first, pltpu.roll(second, 4, axis))
    lower = jnp.where(row < 4, pltpu.roll(first, 4, axis), second)
    return upper, lower


def products_kernel(ids_ref, dev_ref, basis_ref, sens_ref, out_ref, gram_ref, coef_ref, turned_ref):
    step = pl.program_id(0)
    dev = dev_ref[...]
    gram = lax.dot_general(dev, dev, (((0,), (0,)), ((), ())), preferred_element_type=F32)
    coef = jnp.dot(basis_ref[...], dev, preferred_element_type=F32)

    @pl.when(step == 0)
    def _():
        gram_ref[...] = gram
        coef_ref[...] = coef
        turned_ref[...] = sens_ref[...].astype(F32).T
        even = turned_ref[pl.ds(0, ORDER // 2, 2), :]
        odd = turned_ref[pl.ds(1, ORDER // 2, 2), :]
        rows = jnp.concatenate([even, odd], axis=1).reshape(16, 2, 8, 128)
        parts = halves(rows[:, 0], rows[:, 1])
        for x in range(NX):
            for c in range(NC):
                out_ref[2 * x + c, 64:96] = parts[c][4 * x : 4 * x + 4].reshape(32, 128)

    @pl.when(step > 0)
    def _():
        gram_ref[...] += gram
        coef_ref[...] += coef

    @pl.when(step == CHUNKS - 1)
    def _():
        total = gram_ref[...]
        parts = halves(total[:, :128].reshape(32, 8, 128), total[:, 128:].reshape(32, 8, 128))
        for x in range(NX):
            for c in range(NC):
                out_ref[2 * x + c, 0:64] = parts[c][8 * x : 8 * x + 8].reshape(64, 128)
        row = lax.broadcasted_iota(jnp.int32, (BLADES, BLADES), 0)
        col = lax.broadcasted_iota(jnp.int32, (BLADES, BLADES), 1)
        energy = jnp.sum(jnp.where(row == col, total, 0.0), axis=0, keepdims=True)
        table = jnp.concatenate([coef_ref[...], jnp.broadcast_to(energy, (8, BLADES))], axis=0)
        real = lax.broadcasted_iota(jnp.int32, (REAL, BLADES), 0)
        blade = lax.broadcasted_iota(jnp.int32, (REAL, BLADES), 1)
        wanted = jnp.zeros((REAL, BLADES), jnp.int32)
        for r in range(REAL):
            wanted = jnp.where(real == r, ids_ref[r], wanted)
        chosen = (blade == wanted).astype(F32)
        picked = lax.dot_general(
            chosen, table, (((1,), (1,)), ((), ())), precision=HIGHEST, preferred_element_type=F32
        )
        old = lax.broadcasted_iota(jnp.int32, (SHAPES + 8, 128), 0)
        new = lax.broadcasted_iota(jnp.int32, (SHAPES + 8, 128), 1)
        place = jnp.where(old < SHAPES, 8 * ((old // 2) % NY) + 2 * (old // 16) + old % 2, old)
        order = ((place == new) & (old <= SHAPES)).astype(F32)
        picked = jnp.dot(picked, order, precision=HIGHEST, preferred_element_type=F32)
        first, second, third = picked[0:8], picked[8:16], picked[16:24]
        lane = lax.broadcasted_iota(jnp.int32, (8, 128), 1)
        upper = jnp.where(lane < 64, first, pltpu.roll(third, 64, 1))
        lower = jnp.where(lane < 64, second, 0.0)
        lower = jnp.where(lane == 64, first, lower)
        lower = jnp.where(lane == 65, pltpu.roll(second, 1, 1), lower)
        lower = jnp.where(lane == 66, pltpu.roll(third, 2, 1), lower)
        for s in range(NX * NC):
            out_ref[s, 96:104] = upper
            out_ref[s, 104:112] = lower


def products(ids, dev, basis, sens):
    rows = dev.shape[0] // CHUNKS
    return pl.pallas_call(
        products_kernel,
        grid=(CHUNKS,),
        in_specs=[
            SMEM,
            pl.BlockSpec((rows, BLADES), lambda i: (i, 0)),
            pl.BlockSpec((SHAPES, rows), lambda i: (0, i)),
            pl.BlockSpec((SHAPES, ORDER), lambda i: (0, 0)),
        ],
        out_specs=pl.BlockSpec((NX * NC, 112, 128), lambda i: (0, 0, 0)),
        out_shape=jax.ShapeDtypeStruct((NX * NC, 112, 128), F32),
        scratch_shapes=[
            pltpu.VMEM((BLADES, BLADES), F32),
            pltpu.VMEM((SHAPES, BLADES), F32),
            pltpu.VMEM((ORDER, SHAPES), F32),
        ],
        compiler_params=params(32),
        name="products",
    )(ids, dev, basis, sens)


def after_xc_kernel(in_ref, out_ref):
    gram = in_ref[0, 0:64]
    coef = in_ref[0, 96:112]
    for s in range(1, NX * NC):
        gram += in_ref[s, 0:64]
        coef += in_ref[s, 96:112]
    for y in range(NY):
        out_ref[y, 0:8] = gram[8 * y : 8 * y + 8]
        out_ref[y, 8:24] = coef
    for a in range(NX):
        first = in_ref[2 * a, 64:96].reshape(4, 8, 128)
        second = in_ref[2 * a + 1, 64:96].reshape(4, 8, 128)
        parts = halves(first, second)
        for y in range(NY):
            out_ref[y, 24 + 8 * a : 32 + 8 * a] = parts[y % 2][y // 2]


def after_y_kernel(in_ref, out_ref):
    gram = in_ref[0, 0:8]
    coef = in_ref[0, 8:24]
    for y in range(1, NY):
        gram += in_ref[y, 0:8]
        coef += in_ref[y, 8:24]
    row = lax.broadcasted_iota(jnp.int32, (8, 128), 0)
    lane = lax.broadcasted_iota(jnp.int32, (8, 128), 1)
    turned = pltpu.roll(gram, 4, 0)
    for z in range(NZ):
        block = gram if z < 4 else turned
        if z % 4 != 3:
            block = pltpu.roll(block, 96 - 32 * (z % 4), 1)
        out_ref[z, 0:8] = coef[0:8]
        out_ref[z, 8:16] = jnp.where((row < 4) & (lane >= 96), block, coef[8:16])


def final_kernel(points, in_ref, sens_ref, gram_ref, change_ref):
    total = in_ref[0]
    for z in range(1, NZ):
        total += in_ref[z]
    upper, lower = total[0:8], total[8:16]
    gram_ref[...] = pltpu.roll(lower, 32, 1)[0:4, 0:32] / points
    coef = (upper, lower, pltpu.roll(upper, 64, 1))
    weights = []
    for a in range(3):
        energy = lower[:, 64 + a : 65 + a] / points
        weights.append(coef[a][:, 0:SHAPES] / jnp.sqrt(energy + 1e-05))
    weights = jnp.concatenate(weights, axis=0)
    for q in range(4):
        rows = [sens_ref[y, pl.ds(24 + q, 8, 4), :] for y in range(NY)]
        block = jnp.dot(
            weights, jnp.concatenate(rows, axis=0), precision=HIGHEST, preferred_element_type=F32
        )
        change_ref[pl.ds(2 * q, REAL, 8), :] = block[:, 0:64]
        change_ref[pl.ds(2 * q + 1, REAL, 8), :] = block[:, 64:128]


def call(kernel, shape, count, name):
    return pl.pallas_call(
        kernel,
        in_specs=[VMEM] * count,
        out_specs=jax.tree.map(lambda _: VMEM, shape),
        out_shape=shape,
        compiler_params=params(8),
        name=name,
    )


def on_device(deviations, basis, sensitivity, blade_ids):
    points = float(deviations.shape[0] * NX * NY * NC * NZ)
    exchange = functools.partial(lax.all_to_all, split_axis=0, concat_axis=0, tiled=True)
    part = products(blade_ids, deviations, basis.T, sensitivity[0])
    part = exchange(part, ("x", "c"))
    part = call(after_xc_kernel, jax.ShapeDtypeStruct((NY, 56, 128), F32), 1, "after_xc")(part)
    by_y = exchange(part, "y")
    part = call(after_y_kernel, jax.ShapeDtypeStruct((NZ, 16, 128), F32), 1, "after_y")(by_y)
    by_z = exchange(part, "z")
    gram, change = call(
        functools.partial(final_kernel, points),
        (
            jax.ShapeDtypeStruct((4, 32), F32),
            jax.ShapeDtypeStruct((REAL * 8, 64), F32),
        ),
        2,
        "final",
    )(by_z, by_y)
    return gram, change.reshape(REAL, 8, 64).transpose(0, 2, 1)


def solution(mesh):
    fine = Mesh(mesh.devices.reshape(NX, NY, NC, NZ), ("x", "y", "c", "z"))
    pts = ("x", "y", "c")
    rows = P((*pts, "z"), None)
    return jax.shard_map(
        on_device,
        mesh=fine,
        in_specs=(rows, rows, P(pts, "z", None), P()),
        out_specs=(P(pts, "z"), P(None, "z", pts)),
        check_vma=False,
    )
```

time: 673 us -> 59.3 us (0.09)
  the two profiles are of different devices: /device:TPU:16 before, /device:TPU:2 now
where the time goes in v1:
time: 59.3 us; the launch traced here: 59 us
  blocking collectives  49.1 us (83%)
  Pallas kernels  4.74 us (8%)
  local copies, waits for them, and re-layouts  4.51 us (8%)
  between operations  0.65 us (1%)
    all_to_all x1, blocking collectives, on_device(): by_z = exchange(part, 'z')  18.5 us
    all_to_all x1, blocking collectives, on_device(): part = exchange(part, ('x', 'c'))  16.4 us
    all_to_all x1, blocking collectives, on_device(): by_y = exchange(part, 'y')  14.1 us
    unnamed x8, local copies, waits for them, and re-layouts  4.51 us
    pallas_call x1, Pallas kernels, products(): pl.pallas_call(products_kernel, grid=(CHUNKS,), in_specs=[SMEM, pl.BlockS...  3.6 us

profile of v1, /device:TPU:2, one launch (start us, length us, event | category | flops | bytes accessed | tf_op | source)
XLA Modules:
  0.0 59.0 jit_solution(17903286977652555452)
XLA Ops:
  0.6 0.0 copy-start
  0.6 1.9 %copy-done = bf16[6144,256]{1,0:T(8,128)(2,1)S(1)} copy-done((bf16[6144,256]{1,0:T(8,128)(2,1)S(1)}, bf16[6144,256]{1,0:T(8,128)(2,1)}, u32[]{:S(2)}) %copy-start) | copy-done | bytes 3145752
  2.5 0.0 copy-start.1
  2.5 1.1 %copy-done.1 = bf16[6144,64]{0,1:T(8,128)(2,1)S(1)} copy-done((bf16[6144,64]{0,1:T(8,128)(2,1)S(1)}, bf16[6144,64]{0,1:T(8,128)(2,1)}, u32[]{:S(2)}) %copy-start.1) | copy-done | bytes 786456
  3.7 0.0 copy-start.2
  3.7 0.8 %copy-done.2 = bf16[1,64,512]{2,1,0:T(8,128)(2,1)S(1)} copy-done((bf16[1,64,512]{2,1,0:T(8,128)(2,1)S(1)}, bf16[1,64,512]{2,1,0:T(8,128)(2,1)}, u32[]{:S(2)}) %copy-start.2) | copy-done | bytes 65560
  4.5 0.0 copy-start.3
  4.5 0.7 %copy-done.3 = s32[24]{0:T(128)S(1)} copy-done((s32[24]{0:T(128)S(1)}, s32[24]{0:T(128)}, u32[]{:S(2)}) %copy-start.3) | copy-done | bytes 120
  5.2 3.6 %products.1 = f32[8,112,128]{2,1,0:T(8,128)S(1)} custom-call(s32[24]{0:T(128)S(1)} %copy-done.3, bf16[6144,256]{1,0:T(8,128)(2,1)S(1)} %copy-done, bf16[64,6144]{1,0:T(8,128)(2,1)S(1)} %bitcast.5, bf16[64,512]{1,0:T(8,128)(2,1)S(1)} %bitcast.6), custom_call_target="tpu_custom_call" | custom-call | tf_op jit(solution)/shard_map/products/pallas_call | solution.py:95
  8.7 16.4 %all_to_all.15.in_ref = f32[8,112,128]{2,1,0:T(8,128)S(1)} all-to-all(f32[8,112,128]{2,1,0:T(8,128)S(1)} %products.1), channel_id=1, replica_groups=mesh['x'=4,'y'=8,'c'=2,'z'=8] {'x','c'}, dimensions={0} | all-to-all | bytes 917504 | tf_op jit(solution)/shard_map/all_to_all | solution.py:186
  25.2 14.1 %all_to_all.16.in_ref.sens_ref = f32[8,56,128]{2,1,0:T(8,128)S(1)} all-to-all(f32[8,56,128]{2,1,0:T(8,128)S(1)} %after_xc.1), channel_id=1, replica_groups=mesh['x'=4,'y'=8,'c'=2,'z'=8] {'y'}, dimensions={0} | all-to-all | bytes 458752 | tf_op jit(solution)/shard_map/all_to_all | solution.py:188
  39.3 0.1 after_y.1
  39.4 18.5 %all_to_all.17.in_ref = f32[8,16,128]{2,1,0:T(8,128)S(1)} all-to-all(f32[8,16,128]{2,1,0:T(8,128)S(1)} %after_y.1), channel_id=1, replica_groups=mesh['x'=4,'y'=8,'c'=2,'z'=8] {'z'}, dimensions={0} | all-to-all | bytes 131072 | tf_op jit(solution)/shard_map/all_to_all | solution.py:190
  57.9 1.0 %final.1 = (f32[4,32]{1,0:T(4,128)}, f32[192,64]{1,0:T(8,128)}) custom-call(f32[8,16,128]{2,1,0:T(8,128)S(1)} %all_to_all.17.in_ref, f32[8,56,128]{2,1,0:T(8,128)S(1)} %all_to_all.16.in_ref.sens_ref), custom_call_target="tpu_custom_call" | custom-call | tf_op jit(solution)/shard_map/final/pallas_call | solution.py:191
  (1 shorter events, 0.0 us)
Async XLA Ops:
  0.6 1.9 %copy-start = (bf16[6144,256]{1,0:T(8,128)(2,1)S(1)}, bf16[6144,256]{1,0:T(8,128)(2,1)}, u32[]{:S(2)}) copy-start(bf16[6144,256]{1,0:T(8,128)(2,1)} %dev_ref.1) | copy-start | bytes 9437188
  2.5 1.1 %copy-start.1 = (bf16[6144,64]{0,1:T(8,128)(2,1)S(1)}, bf16[6144,64]{0,1:T(8,128)(2,1)}, u32[]{:S(2)}) copy-start(bf16[6144,64]{0,1:T(8,128)(2,1)} %param.5) | copy-start | bytes 2359300
  3.7 0.8 %copy-start.2 = (bf16[1,64,512]{2,1,0:T(8,128)(2,1)S(1)}, bf16[1,64,512]{2,1,0:T(8,128)(2,1)}, u32[]{:S(2)}) copy-start(bf16[1,64,512]{2,1,0:T(8,128)(2,1)} %param.6) | copy-start | bytes 196612
  4.5 0.7 %copy-start.3 = (s32[24]{0:T(128)S(1)}, s32[24]{0:T(128)}, u32[]{:S(2)}) copy-start(s32[24]{0:T(128)} %ids_ref.1) | copy-start | bytes 292

commit v2 on v1

v2 whole, which is shorter than its diff:
```python
import functools

import jax
import jax.numpy as jnp
from jax import lax
from jax.experimental import pallas as pl
from jax.experimental.pallas import tpu as pltpu
from jax.sharding import Mesh, PartitionSpec as P

F32 = jnp.float32
HIGHEST = lax.Precision.HIGHEST
VMEM = pl.BlockSpec(memory_space=pltpu.VMEM)

NX, NY, NC, NZ = 4, 8, 2, 8
BLADES, SHAPES, ORDER, REAL = 256, 64, 512, 24
CHUNKS = 4


def params(mib):
    return pltpu.CompilerParams(vmem_limit_bytes=mib * 1024 * 1024)


def halves(first, second):
    axis = first.ndim - 2
    row = lax.broadcasted_iota(jnp.int32, first.shape, axis)
    upper = jnp.where(row < 4, first, pltpu.roll(second, 4, axis))
    lower = jnp.where(row < 4, pltpu.roll(first, 4, axis), second)
    return upper, lower


def products_kernel(ids_hbm, dev_hbm, basis_hbm, sens_hbm, out_ref, ids_ref, dev_ref, basis_ref, sens_ref, gram_ref, turned_ref, picked_ref, sems):
    rows = dev_ref.shape[0] // CHUNKS
    sens_copy = pltpu.make_async_copy(sens_hbm, sens_ref, sems.at[2 * CHUNKS])
    ids_copy = pltpu.make_async_copy(ids_hbm, ids_ref, sems.at[2 * CHUNKS + 1])
    copies = []
    for i in range(CHUNKS):
        span = pl.ds(i * rows, rows)
        copies.append(pltpu.make_async_copy(dev_hbm.at[span, :], dev_ref.at[span, :], sems.at[2 * i]))
        copies.append(
            pltpu.make_async_copy(basis_hbm.at[:, span], basis_ref.at[:, span], sems.at[2 * i + 1])
        )
    sens_copy.start()
    for copy in copies:
        copy.start()
    ids_copy.start()

    sens_copy.wait()
    turned_ref[0:ORDER, :] = sens_ref[...].astype(F32).T
    even = turned_ref[pl.ds(0, ORDER // 2, 2), :]
    odd = turned_ref[pl.ds(1, ORDER // 2, 2), :]
    tiles = jnp.concatenate([even, odd], axis=1).reshape(16, 2, 8, 128)
    parts = halves(tiles[:, 0], tiles[:, 1])
    for x in range(NX):
        for c in range(NC):
            out_ref[2 * x + c, 64:96] = parts[c][4 * x : 4 * x + 4].reshape(32, 128)

    gram = coef = None
    for i in range(CHUNKS):
        copies[2 * i].wait()
        copies[2 * i + 1].wait()
        dev = dev_ref[i * rows : (i + 1) * rows, :]
        more = lax.dot_general(dev, dev, (((0,), (0,)), ((), ())), preferred_element_type=F32)
        gram = more if gram is None else gram + more
        more = jnp.dot(basis_ref[:, i * rows : (i + 1) * rows], dev, preferred_element_type=F32)
        coef = more if coef is None else coef + more
    gram_ref[...] = gram
    turned_ref[0:BLADES, :] = coef.T
    ids_copy.wait()

    parts = halves(gram[:, :128].reshape(32, 8, 128), gram[:, 128:].reshape(32, 8, 128))
    for x in range(NX):
        for c in range(NC):
            out_ref[2 * x + c, 0:64] = parts[c][8 * x : 8 * x + 8].reshape(64, 128)

    lane = lax.broadcasted_iota(jnp.int32, (1, BLADES), 1)
    for r in range(REAL):
        blade = ids_ref[r]
        picked_ref[r : r + 1, 0:SHAPES] = turned_ref[pl.ds(blade, 1), :]
        row = jnp.where(lane == blade, gram_ref[pl.ds(blade, 1), :], 0.0)
        picked_ref[r : r + 1, 128:256] = row[:, :128] + row[:, 128:]
    coef = [picked_ref[8 * a : 8 * a + 8, 0:128] for a in range(3)]
    energy = [jnp.sum(picked_ref[8 * a : 8 * a + 8, 128:256], axis=1, keepdims=True) for a in range(3)]
    lane = lax.broadcasted_iota(jnp.int32, (8, 128), 1)
    upper = jnp.where(lane < 64, coef[0], pltpu.roll(coef[2], 64, 1))
    lower = jnp.where(lane < 64, coef[1], 0.0)
    for a in range(3):
        lower = jnp.where(lane == 64 + a, energy[a], lower)
    for s in range(NX * NC):
        out_ref[s, 96:104] = upper
        out_ref[s, 104:112] = lower


def products(ids, dev, basis, sens):
    hbm = pl.BlockSpec(memory_space=pltpu.HBM)
    return pl.pallas_call(
        products_kernel,
        in_specs=[hbm] * 4,
        out_specs=VMEM,
        out_shape=jax.ShapeDtypeStruct((NX * NC, 112, 128), F32),
        scratch_shapes=[
            pltpu.SMEM((REAL,), jnp.int32),
            pltpu.VMEM(dev.shape, dev.dtype),
            pltpu.VMEM(basis.shape, basis.dtype),
            pltpu.VMEM(sens.shape, sens.dtype),
            pltpu.VMEM((BLADES, BLADES), F32),
            pltpu.VMEM((ORDER, SHAPES), F32),
            pltpu.VMEM((REAL, 256), F32),
            pltpu.SemaphoreType.DMA((2 * CHUNKS + 2,)),
        ],
        compiler_params=params(24),
        name="products",
    )(*(pltpu.with_memory_space_constraint(v, pltpu.HBM) for v in (ids, dev, basis, sens)))


def after_xc_kernel(in_ref, out_ref):
    gram = in_ref[0, 0:64]
    coef = in_ref[0, 96:112]
    for s in range(1, NX * NC):
        gram += in_ref[s, 0:64]
        coef += in_ref[s, 96:112]
    for y in range(NY):
        out_ref[y, 0:8] = gram[8 * y : 8 * y + 8]
        out_ref[y, 8:24] = coef
    for a in range(NX):
        first = in_ref[2 * a, 64:96].reshape(4, 8, 128)
        second = in_ref[2 * a + 1, 64:96].reshape(4, 8, 128)
        parts = halves(first, second)
        for y in range(NY):
            out_ref[y, 24 + 8 * a : 32 + 8 * a] = parts[y % 2][y // 2]


def after_y_kernel(in_ref, out_ref):
    gram = in_ref[0, 0:8]
    coef = in_ref[0, 8:24]
    for y in range(1, NY):
        gram += in_ref[y, 0:8]
        coef += in_ref[y, 8:24]
    row = lax.broadcasted_iota(jnp.int32, (8, 128), 0)
    lane = lax.broadcasted_iota(jnp.int32, (8, 128), 1)
    turned = pltpu.roll(gram, 4, 0)
    for z in range(NZ):
        block = gram if z < 4 else turned
        if z % 4 != 3:
            block = pltpu.roll(block, 96 - 32 * (z % 4), 1)
        out_ref[z, 0:8] = coef[0:8]
        out_ref[z, 8:16] = jnp.where((row < 4) & (lane >= 96), block, coef[8:16])


def final_kernel(points, in_ref, sens_ref, gram_ref, change_ref, block_ref):
    total = in_ref[0]
    for z in range(1, NZ):
        total += in_ref[z]
    upper, lower = total[0:8], total[8:16]
    gram_ref[...] = pltpu.roll(lower, 32, 1)[0:4, 0:32] / points
    coef = (upper, lower, pltpu.roll(upper, 64, 1))
    weights = []
    for a in range(3):
        energy = lower[:, 64 + a : 65 + a] / points
        weights.append(coef[a][:, 0:SHAPES] / jnp.sqrt(energy + 1e-05))
    weights = jnp.concatenate(weights, axis=0)
    for q in range(4):
        for x in range(NX):
            for c in range(NC):
                block_ref[pl.ds(16 * x + c, NY, 2), :] = sens_ref[
                    pl.ds(24 + 4 * (2 * x + c) + q, NY, 56), :
                ]
        block = jnp.dot(weights, block_ref[...], precision=HIGHEST, preferred_element_type=F32)
        change_ref[pl.ds(2 * q, REAL, 8), :] = block[:, 0:64]
        change_ref[pl.ds(2 * q + 1, REAL, 8), :] = block[:, 64:128]


def call(kernel, shape, count, name, scratch=()):
    return pl.pallas_call(
        kernel,
        in_specs=[VMEM] * count,
        out_specs=jax.tree.map(lambda _: VMEM, shape),
        out_shape=shape,
        scratch_shapes=scratch,
        compiler_params=params(8),
        name=name,
    )


def on_device(deviations, basis, sensitivity, blade_ids):
    points = float(deviations.shape[0] * NX * NY * NC * NZ)
    exchange = functools.partial(lax.all_to_all, split_axis=0, concat_axis=0, tiled=True)
    part = products(blade_ids, deviations, basis.T, sensitivity[0])
    part = exchange(part, ("x", "c"))
    part = call(after_xc_kernel, jax.ShapeDtypeStruct((NY, 56, 128), F32), 1, "after_xc")(part)
    by_y = exchange(part, "y")
    part = call(after_y_kernel, jax.ShapeDtypeStruct((NZ, 16, 128), F32), 1, "after_y")(by_y)
    by_z = exchange(part, "z")
    gram, change = call(
        functools.partial(final_kernel, points),
        (
            jax.ShapeDtypeStruct((4, 32), F32),
            jax.ShapeDtypeStruct((REAL * 8, 64), F32),
        ),
        2,
        "final",
        [pltpu.VMEM((SHAPES, 128), F32)],
    )(by_z, by_y.reshape(NY * 56, 128))
    return gram, change.reshape(REAL, 8, 64).transpose(0, 2, 1)


def solution(mesh):
    fine = Mesh(mesh.devices.reshape(NX, NY, NC, NZ), ("x", "y", "c", "z"))
    pts = ("x", "y", "c")
    rows = P((*pts, "z"), None)
    return jax.shard_map(
        on_device,
        mesh=fine,
        in_specs=(rows, rows, P(pts, "z", None), P()),
        out_specs=(P(pts, "z"), P(None, "z", pts)),
        check_vma=False,
    )
```

time: 59.3 us -> 54.8 us (0.924)
  local copies, waits for them, and re-layouts: 4.51 us -> 0 us
    unnamed x8 -> x0, local copies, waits for them, and re-layouts: 4.51 us -> none
where the time goes in v2:
time: 54.8 us; the launch traced here: 54.6 us
  blocking collectives  49.1 us (90%)
  Pallas kernels  4.86 us (9%)
  between operations  0.64 us (1%)
    all_to_all x1, blocking collectives, on_device(): by_z = exchange(part, 'z')  18.5 us
    all_to_all x1, blocking collectives, on_device(): part = exchange(part, ('x', 'c'))  16.4 us
    all_to_all x1, blocking collectives, on_device(): by_y = exchange(part, 'y')  14.1 us
    pallas_call x1, Pallas kernels, products(): pl.pallas_call(products_kernel, in_specs=[hbm] * 4, out_specs=VMEM, out_s...  3.71 us

profile of v2, /device:TPU:2, one launch (start us, length us, event | category | flops | bytes accessed | tf_op | source)
XLA Modules:
  0.0 54.6 jit_solution(9016619027917294005)
XLA Ops:
  0.6 3.7 %products.1 = f32[8,112,128]{2,1,0:T(8,128)S(1)} custom-call(s32[24]{0:T(128)} %ids_hbm.1, bf16[6144,256]{1,0:T(8,128)(2,1)} %dev_hbm.1, bf16[64,6144]{1,0:T(8,128)(2,1)} %bitcast.7, bf16[64,512]{1,0:T(8,128)(2,1)} %bitcast.8), custom_call_target="tpu_custom_call" | custom-call | tf_op jit(solution)/shard_map/products/pallas_call | solution.py:95
  4.4 16.4 %all_to_all.15.in_ref = f32[8,112,128]{2,1,0:T(8,128)S(1)} all-to-all(f32[8,112,128]{2,1,0:T(8,128)S(1)} %products.1), channel_id=1, replica_groups=mesh['x'=4,'y'=8,'c'=2,'z'=8] {'x','c'}, dimensions={0} | all-to-all | bytes 917504 | tf_op jit(solution)/shard_map/all_to_all | solution.py:188
  20.8 14.1 %all_to_all.16.in_ref = f32[8,56,128]{2,1,0:T(8,128)S(1)} all-to-all(f32[8,56,128]{2,1,0:T(8,128)S(1)} %after_xc.1), channel_id=1, replica_groups=mesh['x'=4,'y'=8,'c'=2,'z'=8] {'y'}, dimensions={0} | all-to-all | bytes 458752 | tf_op jit(solution)/shard_map/all_to_all | solution.py:190
  35.0 0.1 after_y.1
  35.0 18.5 %all_to_all.17.in_ref = f32[8,16,128]{2,1,0:T(8,128)S(1)} all-to-all(f32[8,16,128]{2,1,0:T(8,128)S(1)} %after_y.1), channel_id=1, replica_groups=mesh['x'=4,'y'=8,'c'=2,'z'=8] {'z'}, dimensions={0} | all-to-all | bytes 131072 | tf_op jit(solution)/shard_map/all_to_all | solution.py:192
  53.5 1.0 %final.1 = (f32[4,32]{1,0:T(4,128)}, f32[192,64]{1,0:T(8,128)}) custom-call(f32[8,16,128]{2,1,0:T(8,128)S(1)} %all_to_all.17.in_ref, f32[448,128]{1,0:T(8,128)S(1)} %bitcast.6), custom_call_target="tpu_custom_call" | custom-call | tf_op jit(solution)/shard_map/final/pallas_call | solution.py:193
  (1 shorter events, 0.0 us)

commit v3 on v2

v3 whole, which is shorter than its diff:
```python
import functools

import jax
import jax.numpy as jnp
from jax import lax
from jax.experimental import pallas as pl
from jax.experimental.pallas import tpu as pltpu
from jax.sharding import Mesh, PartitionSpec as P

F32 = jnp.float32
BF16 = jnp.bfloat16
VMEM = pl.BlockSpec(memory_space=pltpu.VMEM)

NX, NY, NC, NZ = 4, 8, 2, 8
BLADES, SHAPES, ORDER, REAL = 256, 64, 512, 24
CHUNKS = (2048, 2048, 2048)


def params(mib):
    return pltpu.CompilerParams(vmem_limit_bytes=mib * 1024 * 1024)


def pair(value):
    high = value.astype(BF16).astype(F32)
    return high, value - high


def halves(first, second):
    axis = first.ndim - 2
    row = lax.broadcasted_iota(jnp.int32, first.shape, axis)
    upper = jnp.where(row < 4, first, pltpu.roll(second, 4, axis))
    lower = jnp.where(row < 4, pltpu.roll(first, 4, axis), second)
    return upper, lower


def products_kernel(ids_hbm, dev_hbm, basis_hbm, sens_hbm, out_ref, ids_ref, dev_ref, basis_ref, sens_ref, gram_ref, turned_ref, picked_ref, sems):
    sens_copy = pltpu.make_async_copy(sens_hbm, sens_ref, sems.at[2 * len(CHUNKS)])
    ids_copy = pltpu.make_async_copy(ids_hbm, ids_ref, sems.at[2 * len(CHUNKS) + 1])
    copies = []
    for i, rows in enumerate(CHUNKS):
        span = pl.ds(sum(CHUNKS[:i]), rows)
        copies.append(pltpu.make_async_copy(dev_hbm.at[span, :], dev_ref.at[span, :], sems.at[2 * i]))
        copies.append(
            pltpu.make_async_copy(basis_hbm.at[:, span], basis_ref.at[:, span], sems.at[2 * i + 1])
        )
    sens_copy.start()
    for copy in copies:
        copy.start()
    ids_copy.start()

    sens_copy.wait()
    turned_ref[0:ORDER, :] = sens_ref[...].astype(F32).T
    even = turned_ref[pl.ds(0, ORDER // 2, 2), :]
    odd = turned_ref[pl.ds(1, ORDER // 2, 2), :]
    tiles = jnp.concatenate([even, odd], axis=1).reshape(16, 2, 8, 128)
    parts = halves(tiles[:, 0], tiles[:, 1])
    for x in range(NX):
        for c in range(NC):
            out_ref[2 * x + c, 160:192] = parts[c][4 * x : 4 * x + 4].reshape(32, 128).astype(BF16)

    gram = coef = None
    for i, rows in enumerate(CHUNKS):
        copies[2 * i].wait()
        copies[2 * i + 1].wait()
        start = sum(CHUNKS[:i])
        dev = dev_ref[start : start + rows, :]
        more = lax.dot_general(dev, dev, (((0,), (0,)), ((), ())), preferred_element_type=F32)
        gram = more if gram is None else gram + more
        more = jnp.dot(basis_ref[:, start : start + rows], dev, preferred_element_type=F32)
        coef = more if coef is None else coef + more
    gram_ref[...] = gram
    turned_ref[0:BLADES, :] = coef.T
    ids_copy.wait()

    parts = halves(gram[:, :128].reshape(32, 8, 128), gram[:, 128:].reshape(32, 8, 128))
    for x in range(NX):
        for c in range(NC):
            high, low = pair(parts[c][8 * x : 8 * x + 8].reshape(64, 128))
            out_ref[2 * x + c, 0:64] = high.astype(BF16)
            out_ref[2 * x + c, 64:128] = low.astype(BF16)

    lane = lax.broadcasted_iota(jnp.int32, (1, BLADES), 1)
    for r in range(REAL):
        blade = ids_ref[r]
        picked_ref[r : r + 1, 0:SHAPES] = turned_ref[pl.ds(blade, 1), :]
        row = jnp.where(lane == blade, gram_ref[pl.ds(blade, 1), :], 0.0)
        picked_ref[r : r + 1, 128:256] = row[:, :128] + row[:, 128:]
    coef = [picked_ref[8 * a : 8 * a + 8, 0:128] for a in range(3)]
    energy = [jnp.sum(picked_ref[8 * a : 8 * a + 8, 128:256], axis=1, keepdims=True) for a in range(3)]
    lane = lax.broadcasted_iota(jnp.int32, (8, 128), 1)
    upper = jnp.where(lane < 64, coef[0], pltpu.roll(coef[2], 64, 1))
    lower = jnp.where(lane < 64, coef[1], 0.0)
    for a in range(3):
        lower = jnp.where(lane == 64 + a, energy[a], lower)
    high, low = pair(jnp.concatenate([upper, lower], axis=0))
    for s in range(NX * NC):
        out_ref[s, 128:144] = high.astype(BF16)
        out_ref[s, 144:160] = low.astype(BF16)


def products(ids, dev, basis, sens):
    hbm = pl.BlockSpec(memory_space=pltpu.HBM)
    return pl.pallas_call(
        products_kernel,
        in_specs=[hbm] * 4,
        out_specs=VMEM,
        out_shape=jax.ShapeDtypeStruct((NX * NC, 192, 128), BF16),
        scratch_shapes=[
            pltpu.SMEM((REAL,), jnp.int32),
            pltpu.VMEM(dev.shape, dev.dtype),
            pltpu.VMEM(basis.shape, basis.dtype),
            pltpu.VMEM(sens.shape, sens.dtype),
            pltpu.VMEM((BLADES, BLADES), F32),
            pltpu.VMEM((ORDER, SHAPES), F32),
            pltpu.VMEM((REAL, 256), F32),
            pltpu.SemaphoreType.DMA((2 * len(CHUNKS) + 2,)),
        ],
        compiler_params=params(24),
        name="products",
    )(*(pltpu.with_memory_space_constraint(v, pltpu.HBM) for v in (ids, dev, basis, sens)))


def after_xc_kernel(in_ref, out_ref):
    gram = coef = 0.0
    for s in range(NX * NC):
        gram += in_ref[s, 0:64].astype(F32) + in_ref[s, 64:128].astype(F32)
        coef += in_ref[s, 128:144].astype(F32) + in_ref[s, 144:160].astype(F32)
    gram_high, gram_low = pair(gram)
    coef_high, coef_low = pair(coef)
    tiles = [in_ref[s, 160:192].astype(F32).reshape(4, 8, 128) for s in range(NX * NC)]
    parts = [halves(tiles[2 * a], tiles[2 * a + 1]) for a in range(NX)]
    for y in range(NY):
        rows = slice(8 * y, 8 * y + 8)
        out_ref[y, 0:16] = jnp.concatenate([gram_high[rows], gram_low[rows]], axis=0).astype(BF16)
        out_ref[y, 16:32] = coef_high.astype(BF16)
        out_ref[y, 32:48] = coef_low.astype(BF16)
        sens = [parts[a][y % 2][y // 2] for a in range(NX)]
        out_ref[y, 48:80] = jnp.concatenate(sens, axis=0).astype(BF16)


def after_y_kernel(in_ref, out_ref, sens_ref, rows_ref, block_ref):
    gram = coef = 0.0
    for y in range(NY):
        both = in_ref[y, 0:16].astype(F32)
        gram += both[0:8] + both[8:16]
        coef += in_ref[y, 16:32].astype(F32) + in_ref[y, 32:48].astype(F32)
        rows_ref[32 * y : 32 * y + 32, :] = in_ref[y, 48:80].astype(F32)
    row = lax.broadcasted_iota(jnp.int32, (8, 128), 0)
    lane = lax.broadcasted_iota(jnp.int32, (8, 128), 1)
    turned = pltpu.roll(gram, 4, 0)
    for z in range(NZ):
        block = gram if z < 4 else turned
        if z % 4 != 3:
            block = pltpu.roll(block, 96 - 32 * (z % 4), 1)
        out_ref[z, 0:8] = coef[0:8]
        out_ref[z, 8:16] = jnp.where((row < 4) & (lane >= 96), block, coef[8:16])
    for q in range(4):
        for s in range(NX * NC):
            first = 16 * (s // 2) + s % 2
            block_ref[q, pl.ds(first, NY, 2), :] = rows_ref[pl.ds(4 * s + q, NY, 32), :]
    sens_ref[...] = block_ref[...].astype(BF16)


def final_kernel(points, in_ref, sens_ref, gram_ref, change_ref):
    total = in_ref[0]
    for z in range(1, NZ):
        total += in_ref[z]
    upper, lower = total[0:8], total[8:16]
    gram_ref[...] = pltpu.roll(lower, 32, 1)[0:4, 0:32] / points
    coef = (upper, lower, pltpu.roll(upper, 64, 1))
    weights = []
    for a in range(3):
        energy = lower[:, 64 + a : 65 + a] / points
        weights.append(coef[a][:, 0:SHAPES] / jnp.sqrt(energy + 1e-05))
    high, rest = pair(jnp.concatenate(weights, axis=0))
    middle, low = pair(rest)
    terms = jnp.concatenate([high, middle, low], axis=0).astype(BF16)
    for q in range(4):
        block = jnp.dot(terms, sens_ref[q], preferred_element_type=F32)
        block = block[0:REAL] + (block[REAL : 2 * REAL] + block[2 * REAL :])
        change_ref[pl.ds(2 * q, REAL, 8), :] = block[:, 0:64]
        change_ref[pl.ds(2 * q + 1, REAL, 8), :] = block[:, 64:128]


def call(kernel, shape, count, name, scratch=()):
    return pl.pallas_call(
        kernel,
        in_specs=[VMEM] * count,
        out_specs=jax.tree.map(lambda _: VMEM, shape),
        out_shape=shape,
        scratch_shapes=scratch,
        compiler_params=params(8),
        name=name,
    )


def on_device(deviations, basis, sensitivity, blade_ids):
    points = float(deviations.shape[0] * NX * NY * NC * NZ)
    exchange = functools.partial(lax.all_to_all, split_axis=0, concat_axis=0, tiled=True)
    part = products(blade_ids, deviations, basis.T, sensitivity[0])
    part = exchange(part, ("x", "c"))
    part = call(after_xc_kernel, jax.ShapeDtypeStruct((NY, 80, 128), BF16), 1, "after_xc")(part)
    part = exchange(part, "y")
    part, sens = call(
        after_y_kernel,
        (
            jax.ShapeDtypeStruct((NZ, 16, 128), F32),
            jax.ShapeDtypeStruct((4, SHAPES, 128), BF16),
        ),
        1,
        "after_y",
        [pltpu.VMEM((NY * 32, 128), F32), pltpu.VMEM((4, SHAPES, 128), F32)],
    )(part)
    part = exchange(part, "z")
    gram, change = call(
        functools.partial(final_kernel, points),
        (
            jax.ShapeDtypeStruct((4, 32), F32),
            jax.ShapeDtypeStruct((REAL * 8, 64), F32),
        ),
        2,
        "final",
    )(part, sens)
    return gram, change.reshape(REAL, 8, 64).transpose(0, 2, 1)


def solution(mesh):
    fine = Mesh(mesh.devices.reshape(NX, NY, NC, NZ), ("x", "y", "c", "z"))
    pts = ("x", "y", "c")
    rows = P((*pts, "z"), None)
    return jax.shard_map(
        on_device,
        mesh=fine,
        in_specs=(rows, rows, P(pts, "z", None), P()),
        out_specs=(P(pts, "z"), P(None, "z", pts)),
        check_vma=False,
    )
```

time: 54.8 us -> 52.8 us (0.964)
  blocking collectives: 49.1 us -> 47.1 us
    all_to_all x2, blocking collectives: 32.6 us -> 31.3 us  [the longest x1 18.5 us: on_device(): part = exchange(part, 'z')]
    all_to_all x1, blocking collectives: 16.4 us -> 15.7 us  [on_device(): part = exchange(part, ('x', 'c'))]
where the time goes in v3:
time: 52.8 us; the launch traced here: 52.6 us
  blocking collectives  47.1 us (89%)
  Pallas kernels  4.89 us (9%)
  between operations  0.64 us (1%)
    all_to_all x1, blocking collectives, on_device(): part = exchange(part, 'z')  18.5 us
    all_to_all x1, blocking collectives, on_device(): part = exchange(part, ('x', 'c'))  15.7 us
    all_to_all x1, blocking collectives, on_device(): part = exchange(part, 'y')  12.8 us
    pallas_call x1, Pallas kernels, products(): pl.pallas_call(products_kernel, in_specs=[hbm] * 4, out_specs=VMEM, out_s...  3.74 us

profile of v3, /device:TPU:2, one launch (start us, length us, event | category | flops | bytes accessed | tf_op | source)
XLA Modules:
  0.0 52.6 jit_solution(12454914575783390600)
XLA Ops:
  0.6 3.7 %products.1 = bf16[8,192,128]{2,1,0:T(8,128)(2,1)S(1)} custom-call(s32[24]{0:T(128)} %ids_hbm.1, bf16[6144,256]{1,0:T(8,128)(2,1)} %dev_hbm.1, bf16[64,6144]{1,0:T(8,128)(2,1)} %bitcast.5, bf16[64,512]{1,0:T(8,128)(2,1)} %bitcast.6), custom_call_target="tpu_custom_call" | custom-call | tf_op jit(solution)/shard_map/products/pallas_call | solution.py:103
  4.4 15.7 %all_to_all.15.in_ref = bf16[8,192,128]{2,1,0:T(8,128)(2,1)S(1)} all-to-all(bf16[8,192,128]{2,1,0:T(8,128)(2,1)S(1)} %products.1), channel_id=1, replica_groups=mesh['x'=4,'y'=8,'c'=2,'z'=8] {'x','c'}, dimensions={0} | all-to-all | bytes 786432 | tf_op jit(solution)/shard_map/all_to_all | solution.py:201
  20.1 0.1 after_xc.1
  20.2 12.8 %all_to_all.16.in_ref = bf16[8,80,128]{2,1,0:T(8,128)(2,1)S(1)} all-to-all(bf16[8,80,128]{2,1,0:T(8,128)(2,1)S(1)} %after_xc.1), channel_id=1, replica_groups=mesh['x'=4,'y'=8,'c'=2,'z'=8] {'y'}, dimensions={0} | all-to-all | bytes 327680 | tf_op jit(solution)/shard_map/all_to_all | solution.py:203
  33.0 0.1 after_y.1
  33.1 18.5 %all_to_all.17.in_ref = f32[8,16,128]{2,1,0:T(8,128)S(1)} all-to-all(f32[8,16,128]{2,1,0:T(8,128)S(1)} %get-tuple-element.6), channel_id=1, replica_groups=mesh['x'=4,'y'=8,'c'=2,'z'=8] {'z'}, dimensions={0} | all-to-all | bytes 131072 | tf_op jit(solution)/shard_map/all_to_all | solution.py:214
  51.6 1.0 %final.1 = (f32[4,32]{1,0:T(4,128)}, f32[192,64]{1,0:T(8,128)}) custom-call(f32[8,16,128]{2,1,0:T(8,128)S(1)} %all_to_all.17.in_ref, bf16[4,64,128]{2,1,0:T(8,128)(2,1)S(1)} %get-tuple-element.7.sens_ref), custom_call_target="tpu_custom_call" | custom-call | tf_op jit(solution)/shard_map/final/pallas_call | solution.py:215

commit v4 on v3

--- a/solution.py
+++ b/solution.py
@@ -13,7 +13,7 @@
 
 NX, NY, NC, NZ = 4, 8, 2, 8
 BLADES, SHAPES, ORDER, REAL = 256, 64, 512, 24
-CHUNKS = (2048, 2048, 2048)
+CHUNKS = (2048, 4096)
 
 
 def params(mib):
@@ -58,18 +58,18 @@
         for c in range(NC):
             out_ref[2 * x + c, 160:192] = parts[c][4 * x : 4 * x + 4].reshape(32, 128).astype(BF16)
 
-    gram = coef = None
+    total = None
     for i, rows in enumerate(CHUNKS):
         copies[2 * i].wait()
         copies[2 * i + 1].wait()
         start = sum(CHUNKS[:i])
         dev = dev_ref[start : start + rows, :]
-        more = lax.dot_general(dev, dev, (((0,), (0,)), ((), ())), preferred_element_type=F32)
-        gram = more if gram is None else gram + more
-        more = jnp.dot(basis_ref[:, start : start + rows], dev, preferred_element_type=F32)
-        coef = more if coef is None else coef + more
+        left = jnp.concatenate([dev.T, basis_ref[:, start : start + rows]], axis=0)
+        more = jnp.dot(left, dev, preferred_element_type=F32)
+        total = more if total is None else total + more
+    gram = total[0:BLADES]
     gram_ref[...] = gram
-    turned_ref[0:BLADES, :] = coef.T
+    turned_ref[0:BLADES, :] = total[BLADES:].T
     ids_copy.wait()
 
     parts = halves(gram[:, :128].reshape(32, 8, 128), gram[:, 128:].reshape(32, 8, 128))

time: 52.8 us -> 52.7 us (level)
  no operation moved by 1% of the time
where the time goes in v4:
time: 52.7 us; the launch traced here: 52.4 us
  blocking collectives  47 us (89%)
  Pallas kernels  4.76 us (9%)
  between operations  0.64 us (1%)
    all_to_all x1, blocking collectives, on_device(): part = exchange(part, 'z')  18.5 us
    all_to_all x1, blocking collectives, on_device(): part = exchange(part, ('x', 'c'))  15.7 us
    all_to_all x1, blocking collectives, on_device(): part = exchange(part, 'y')  12.8 us
    pallas_call x1, Pallas kernels, products(): pl.pallas_call(products_kernel, in_specs=[hbm] * 4, out_specs=VMEM, out_s...  3.61 us

profile of v4, /device:TPU:2, one launch (start us, length us, event | category | flops | bytes accessed | tf_op | source)
XLA Modules:
  0.0 52.4 jit_solution(10477810180880586324)
XLA Ops:
  0.6 3.6 %products.1 = bf16[8,192,128]{2,1,0:T(8,128)(2,1)S(1)} custom-call(s32[24]{0:T(128)} %ids_hbm.1, bf16[6144,256]{1,0:T(8,128)(2,1)} %dev_hbm.1, bf16[64,6144]{1,0:T(8,128)(2,1)} %bitcast.5, bf16[64,512]{1,0:T(8,128)(2,1)} %bitcast.6), custom_call_target="tpu_custom_call" | custom-call | tf_op jit(solution)/shard_map/products/pallas_call | solution.py:103
  4.2 15.7 %all_to_all.15.in_ref = bf16[8,192,128]{2,1,0:T(8,128)(2,1)S(1)} all-to-all(bf16[8,192,128]{2,1,0:T(8,128)(2,1)S(1)} %products.1), channel_id=1, replica_groups=mesh['x'=4,'y'=8,'c'=2,'z'=8] {'x','c'}, dimensions={0} | all-to-all | bytes 786432 | tf_op jit(solution)/shard_map/all_to_all | solution.py:201
  20.0 0.1 after_xc.1
  20.0 12.8 %all_to_all.16.in_ref = bf16[8,80,128]{2,1,0:T(8,128)(2,1)S(1)} all-to-all(bf16[8,80,128]{2,1,0:T(8,128)(2,1)S(1)} %after_xc.1), channel_id=1, replica_groups=mesh['x'=4,'y'=8,'c'=2,'z'=8] {'y'}, dimensions={0} | all-to-all | bytes 327680 | tf_op jit(solution)/shard_map/all_to_all | solution.py:203
  32.9 0.1 after_y.1
  33.0 18.5 %all_to_all.17.in_ref = f32[8,16,128]{2,1,0:T(8,128)S(1)} all-to-all(f32[8,16,128]{2,1,0:T(8,128)S(1)} %get-tuple-element.6), channel_id=1, replica_groups=mesh['x'=4,'y'=8,'c'=2,'z'=8] {'z'}, dimensions={0} | all-to-all | bytes 131072 | tf_op jit(solution)/shard_map/all_to_all | solution.py:214
  51.5 1.0 %final.1 = (f32[4,32]{1,0:T(4,128)}, f32[192,64]{1,0:T(8,128)}) custom-call(f32[8,16,128]{2,1,0:T(8,128)S(1)} %all_to_all.17.in_ref, bf16[4,64,128]{2,1,0:T(8,128)(2,1)S(1)} %get-tuple-element.7.sens_ref), custom_call_target="tpu_custom_call" | custom-call | tf_op jit(solution)/shard_map/final/pallas_call | solution.py:215

commit v5 on v4

--- a/solution.py
+++ b/solution.py
@@ -13,7 +13,7 @@
 
 NX, NY, NC, NZ = 4, 8, 2, 8
 BLADES, SHAPES, ORDER, REAL = 256, 64, 512, 24
-CHUNKS = (2048, 4096)
+CHUNKS = (3072,) * 2
 
 
 def params(mib):
@@ -33,7 +33,7 @@
     return upper, lower
 
 
-def products_kernel(ids_hbm, dev_hbm, basis_hbm, sens_hbm, out_ref, ids_ref, dev_ref, basis_ref, sens_ref, gram_ref, turned_ref, picked_ref, sems):
+def products_kernel(ids_hbm, dev_hbm, basis_hbm, sens_hbm, out_ref, ids_ref, dev_ref, basis_ref, sens_ref, total_ref, turned_ref, picked_ref, sems):
     sens_copy = pltpu.make_async_copy(sens_hbm, sens_ref, sems.at[2 * len(CHUNKS)])
     ids_copy = pltpu.make_async_copy(ids_hbm, ids_ref, sems.at[2 * len(CHUNKS) + 1])
     copies = []
@@ -48,6 +48,7 @@
         copy.start()
     ids_copy.start()
 
+    total_ref[...] = jnp.zeros_like(total_ref)
     sens_copy.wait()
     turned_ref[0:ORDER, :] = sens_ref[...].astype(F32).T
     even = turned_ref[pl.ds(0, ORDER // 2, 2), :]
@@ -58,18 +59,21 @@
         for c in range(NC):
             out_ref[2 * x + c, 160:192] = parts[c][4 * x : 4 * x + 4].reshape(32, 128).astype(BF16)
 
-    total = None
-    for i, rows in enumerate(CHUNKS):
-        copies[2 * i].wait()
-        copies[2 * i + 1].wait()
-        start = sum(CHUNKS[:i])
-        dev = dev_ref[start : start + rows, :]
-        left = jnp.concatenate([dev.T, basis_ref[:, start : start + rows]], axis=0)
+    rows = CHUNKS[0]
+
+    def step(i, carry):
+        span = pl.ds(pl.multiple_of(i * rows, rows), rows)
+        pltpu.make_async_copy(dev_hbm.at[span, :], dev_ref.at[span, :], sems.at[2 * i]).wait()
+        pltpu.make_async_copy(basis_hbm.at[:, span], basis_ref.at[:, span], sems.at[2 * i + 1]).wait()
+        dev = dev_ref[span, :]
+        left = jnp.concatenate([dev.T, basis_ref[:, span]], axis=0)
         more = jnp.dot(left, dev, preferred_element_type=F32)
-        total = more if total is None else total + more
-    gram = total[0:BLADES]
-    gram_ref[...] = gram
-    turned_ref[0:BLADES, :] = total[BLADES:].T
+        total_ref[...] += more
+        return carry
+
+    lax.fori_loop(0, len(CHUNKS), step, 0)
+    gram = total_ref[0:BLADES]
+    turned_ref[0:BLADES, :] = total_ref[BLADES:, :].T
     ids_copy.wait()
 
     parts = halves(gram[:, :128].reshape(32, 8, 128), gram[:, 128:].reshape(32, 8, 128))
@@ -83,7 +87,7 @@
     for r in range(REAL):
         blade = ids_ref[r]
         picked_ref[r : r + 1, 0:SHAPES] = turned_ref[pl.ds(blade, 1), :]
-        row = jnp.where(lane == blade, gram_ref[pl.ds(blade, 1), :], 0.0)
+        row = jnp.where(lane == blade, total_ref[pl.ds(blade, 1), :], 0.0)
         picked_ref[r : r + 1, 128:256] = row[:, :128] + row[:, 128:]
     coef = [picked_ref[8 * a : 8 * a + 8, 0:128] for a in range(3)]
     energy = [jnp.sum(picked_ref[8 * a : 8 * a + 8, 128:256], axis=1, keepdims=True) for a in range(3)]
@@ -110,7 +114,7 @@
             pltpu.VMEM(dev.shape, dev.dtype),
             pltpu.VMEM(basis.shape, basis.dtype),
             pltpu.VMEM(sens.shape, sens.dtype),
-            pltpu.VMEM((BLADES, BLADES), F32),
+            pltpu.VMEM((BLADES + SHAPES, BLADES), F32),
             pltpu.VMEM((ORDER, SHAPES), F32),
             pltpu.VMEM((REAL, 256), F32),
             pltpu.SemaphoreType.DMA((2 * len(CHUNKS) + 2,)),

time: 52.7 us -> 52.3 us (level)
  no operation moved by 1% of the time
where the time goes in v5:
time: 52.3 us; the launch traced here: 52.1 us
  blocking collectives  47 us (90%)
  Pallas kernels  4.39 us (8%)
  between operations  0.64 us (1%)
    all_to_all x1, blocking collectives, on_device(): part = exchange(part, 'z')  18.5 us
    all_to_all x1, blocking collectives, on_device(): part = exchange(part, ('x', 'c'))  15.7 us
    all_to_all x1, blocking collectives, on_device(): part = exchange(part, 'y')  12.8 us
    pallas_call x1, Pallas kernels, products(): pl.pallas_call(products_kernel, in_specs=[hbm] * 4, out_specs=VMEM, out_s...  3.24 us

profile of v5, /device:TPU:2, one launch (start us, length us, event | category | flops | bytes accessed | tf_op | source)
XLA Modules:
  0.0 52.1 jit_solution(7355102470922074706)
XLA Ops:
  0.6 3.2 %products.1 = bf16[8,192,128]{2,1,0:T(8,128)(2,1)S(1)} custom-call(s32[24]{0:T(128)} %ids_hbm.1, bf16[6144,256]{1,0:T(8,128)(2,1)} %dev_hbm.1, bf16[64,6144]{1,0:T(8,128)(2,1)} %bitcast.5, bf16[64,512]{1,0:T(8,128)(2,1)} %bitcast.6), custom_call_target="tpu_custom_call" | custom-call | tf_op jit(solution)/shard_map/products/pallas_call | solution.py:107
  3.9 15.7 %all_to_all.15.in_ref = bf16[8,192,128]{2,1,0:T(8,128)(2,1)S(1)} all-to-all(bf16[8,192,128]{2,1,0:T(8,128)(2,1)S(1)} %products.1), channel_id=1, replica_groups=mesh['x'=4,'y'=8,'c'=2,'z'=8] {'x','c'}, dimensions={0} | all-to-all | bytes 786432 | tf_op jit(solution)/shard_map/all_to_all | solution.py:205
  19.6 0.1 after_xc.1
  19.7 12.8 %all_to_all.16.in_ref = bf16[8,80,128]{2,1,0:T(8,128)(2,1)S(1)} all-to-all(bf16[8,80,128]{2,1,0:T(8,128)(2,1)S(1)} %after_xc.1), channel_id=1, replica_groups=mesh['x'=4,'y'=8,'c'=2,'z'=8] {'y'}, dimensions={0} | all-to-all | bytes 327680 | tf_op jit(solution)/shard_map/all_to_all | solution.py:207
  32.5 0.1 after_y.1
  32.6 18.5 %all_to_all.17.in_ref = f32[8,16,128]{2,1,0:T(8,128)S(1)} all-to-all(f32[8,16,128]{2,1,0:T(8,128)S(1)} %get-tuple-element.6), channel_id=1, replica_groups=mesh['x'=4,'y'=8,'c'=2,'z'=8] {'z'}, dimensions={0} | all-to-all | bytes 131072 | tf_op jit(solution)/shard_map/all_to_all | solution.py:218
  51.1 1.0 %final.1 = (f32[4,32]{1,0:T(4,128)}, f32[192,64]{1,0:T(8,128)}) custom-call(f32[8,16,128]{2,1,0:T(8,128)S(1)} %all_to_all.17.in_ref, bf16[4,64,128]{2,1,0:T(8,128)(2,1)S(1)} %get-tuple-element.7.sens_ref), custom_call_target="tpu_custom_call" | custom-call | tf_op jit(solution)/shard_map/final/pallas_call | solution.py:219

commit v6 on v5

--- a/solution.py
+++ b/solution.py
@@ -44,7 +44,7 @@
             pltpu.make_async_copy(basis_hbm.at[:, span], basis_ref.at[:, span], sems.at[2 * i + 1])
         )
     sens_copy.start()
-    for copy in copies:
+    for copy in copies[1::2] + copies[::2]:
         copy.start()
     ids_copy.start()
 

time: 52.3 us -> 52.5 us (level)
  no operation moved by 1% of the time
where the time goes in v6:
time: 52.5 us; the launch traced here: 52.3 us
  blocking collectives  47 us (90%)
  Pallas kernels  4.57 us (9%)
  between operations  0.64 us (1%)
    all_to_all x1, blocking collectives, on_device(): part = exchange(part, 'z')  18.5 us
    all_to_all x1, blocking collectives, on_device(): part = exchange(part, ('x', 'c'))  15.7 us
    all_to_all x1, blocking collectives, on_device(): part = exchange(part, 'y')  12.8 us
    pallas_call x1, Pallas kernels, products(): pl.pallas_call(products_kernel, in_specs=[hbm] * 4, out_specs=VMEM, out_s...  3.42 us

profile of v6, /device:TPU:2, one launch (start us, length us, event | category | flops | bytes accessed | tf_op | source)
XLA Modules:
  0.0 52.3 jit_solution(16438107758964441639)
XLA Ops:
  0.6 3.4 %products.1 = bf16[8,192,128]{2,1,0:T(8,128)(2,1)S(1)} custom-call(s32[24]{0:T(128)} %ids_hbm.1, bf16[6144,256]{1,0:T(8,128)(2,1)} %dev_hbm.1, bf16[64,6144]{1,0:T(8,128)(2,1)} %bitcast.5, bf16[64,512]{1,0:T(8,128)(2,1)} %bitcast.6), custom_call_target="tpu_custom_call" | custom-call | tf_op jit(solution)/shard_map/products/pallas_call | solution.py:107
  4.1 15.7 %all_to_all.15.in_ref = bf16[8,192,128]{2,1,0:T(8,128)(2,1)S(1)} all-to-all(bf16[8,192,128]{2,1,0:T(8,128)(2,1)S(1)} %products.1), channel_id=1, replica_groups=mesh['x'=4,'y'=8,'c'=2,'z'=8] {'x','c'}, dimensions={0} | all-to-all | bytes 786432 | tf_op jit(solution)/shard_map/all_to_all | solution.py:205
  19.8 0.1 after_xc.1
  19.9 12.8 %all_to_all.16.in_ref = bf16[8,80,128]{2,1,0:T(8,128)(2,1)S(1)} all-to-all(bf16[8,80,128]{2,1,0:T(8,128)(2,1)S(1)} %after_xc.1), channel_id=1, replica_groups=mesh['x'=4,'y'=8,'c'=2,'z'=8] {'y'}, dimensions={0} | all-to-all | bytes 327680 | tf_op jit(solution)/shard_map/all_to_all | solution.py:207
  32.7 0.1 after_y.1
  32.8 18.5 %all_to_all.17.in_ref = f32[8,16,128]{2,1,0:T(8,128)S(1)} all-to-all(f32[8,16,128]{2,1,0:T(8,128)S(1)} %get-tuple-element.6), channel_id=1, replica_groups=mesh['x'=4,'y'=8,'c'=2,'z'=8] {'z'}, dimensions={0} | all-to-all | bytes 131072 | tf_op jit(solution)/shard_map/all_to_all | solution.py:218
  51.3 1.0 %final.1 = (f32[4,32]{1,0:T(4,128)}, f32[192,64]{1,0:T(8,128)}) custom-call(f32[8,16,128]{2,1,0:T(8,128)S(1)} %all_to_all.17.in_ref, bf16[4,64,128]{2,1,0:T(8,128)(2,1)S(1)} %get-tuple-element.7.sens_ref), custom_call_target="tpu_custom_call" | custom-call | tf_op jit(solution)/shard_map/final/pallas_call | solution.py:219
